TPU v7x, 256 devices: a whole 4x4x8 slice. The times are simulated.
256 devices in a mesh: section: 16 (over z, core), expert: 16 (over x, y).
Axes of the slice: x: 4, y: 4, z: 8, core: 2. Of those that a mesh axis runs over, the one named last changes fastest.
Arguments:
- left_in: bfloat16 [16, 1024, 2048], P('section', 'expert'), may hold values from -6 to 6
- left_new: bfloat16 [1024, 2048], P('expert'), may hold values from -6 to 6
- left_saved: bfloat16 [16, 1024, 2048], P('section', 'expert'), may hold values from -6 to 6
- left_cot: bfloat16 [16, 1024, 2048], P('section', 'expert'), may hold values from -6 to 6
- right_in: bfloat16 [16, 1024, 2048], P('section', 'expert'), may hold values from -6 to 6
- right_saved: bfloat16 [2, 16, 1024, 2048], P(None, 'section', 'expert'), may hold values from -6 to 6
- right_cot: bfloat16 [16, 1024, 2048], P('section', 'expert'), may hold values from -6 to 6
- right_cot_new: bfloat16 [1024, 2048], P('expert'), may hold values from -6 to 6
- expert_ids: int32 [3, 2, 16, 1024, 1], P(None, None, 'section', 'expert'), may hold values from 0 to 7; in each aligned block of 64 rows (0 to 63, 64 to 127, ..., all dimensions but the last counted through in order) at most 10 rows name the same one
- gate_values: float32 [3, 2, 16, 1024, 1], P(None, None, 'section', 'expert'), may hold values from 0.25 to 1
- w_gate: bfloat16 [16, 16, 2048, 384], P('section', 'expert'), may hold values from -0.125 to 0.125
- w_up: bfloat16 [16, 16, 2048, 384], P('section', 'expert'), may hold values from -0.125 to 0.125
- w_down: bfloat16 [16, 16, 384, 2048], P('section', 'expert'), may hold values from -0.21875 to 0.21875
Outputs:
- left_out: bfloat16 [2, 16, 1024, 2048], P(None, 'section', 'expert')
- right_out: bfloat16 [16, 1024, 2048], P('section', 'expert')
- left_back: bfloat16 [16, 1024, 2048], P('section', 'expert')
- right_back: bfloat16 [2, 16, 1024, 2048], P(None, 'section', 'expert')
- grad_gate: bfloat16 [16, 16, 2048, 384], P('section', 'expert')
- grad_up: bfloat16 [16, 16, 2048, 384], P('section', 'expert')
- grad_down: bfloat16 [16, 16, 384, 2048], P('section', 'expert')
Inputs may be any that keep to these rules, and one draw needn't show every extreme that they name: `expert_ids`: each row names one expert. In each aligned block of 64 rows (one device's tokens in one pass) no expert is named by more than 10 rows, and in some blocks one expert is named by exactly 10 rows.
All inputs are finite; a program needn't handle non-finite values.
Results may differ from a plain program's by a relative error of at most 0.0064.
Values may be sent and summed in bfloat16 or wider, within the bound.
A program may use at most 128 MiB of HBM per device.

v0:
```python
import jax
import jax.numpy as jnp
from jax import lax
from jax.experimental import pallas as pl
from jax.experimental.pallas import tpu as pltpu
from jax.sharding import PartitionSpec as P

BF = jnp.bfloat16
F32 = jnp.float32
MESH = pl.DeviceIdType.MESH
TOK = 64
D = 2048
HALF = 384
SLAB = 2560
CHUNK = 512
ROWS = 160

F0, B0, F1, B1, F2, B2 = range(6)
U_F0, U_B1X, U_B1C, U_B0X, U_B0C, U_F1, U_B2X, U_F2, U_B2C = range(9)


def iota(shape, dim):
    return lax.broadcasted_iota(jnp.int32, shape, dim)


def dot(a, b):
    return jnp.dot(a, b, preferred_element_type=F32)


def dot_nt(a, b):
    return lax.dot_general(a, b, (((1,), (1,)), ((), ())), preferred_element_type=F32)


def dot_tn(a, b):
    return lax.dot_general(a, b, (((0,), (0,)), ((), ())), preferred_element_type=F32)


def kernel(
    ids_ref,
    gates_ref,
    left_in,
    left_new,
    left_saved,
    left_cot,
    right_in,
    right_saved,
    right_cot,
    right_cot_new,
    w_gate,
    w_up,
    w_down,
    left_out,
    right_out,
    left_back,
    right_back,
    grad_gate,
    grad_up,
    grad_down,
    ptab,
    pttab,
    gtab,
    wgu,
    wd,
    tok,
    mir,
    passed,
    outs,
    send,
    recv,
    part,
    half,
    sums,
    vals,
    xall,
    call,
    dgu,
    hid,
    xfwd,
    gg_buf,
    gu_buf,
    gd_buf,
    load_sem,
    mir_sem,
    s1_send,
    s1_recv,
    rl_send,
    rl_recv,
    pt_send,
    pt_recv,
    sm_send,
    sm_recv,
    ps_sem,
    out_sem,
):
    sec = lax.axis_index("section")
    me = lax.axis_index("expert")
    x = lax.div(me, 4)
    y = lax.rem(me, 4)
    pair = lax.div(y, 2)
    partner = x * 4 + (y + 1 - 2 * lax.rem(y, 2))
    mine = 2 * x + pair
    mirror = 15 - sec
    after = lax.rem(sec + 1, 16)
    ahead = lax.rem(sec + 15, 16)

    peers = []
    for step in (2, 1, 3, 0):
        xd = lax.rem(x + step, 4)
        for a in (1, 0):
            if step == 0 and a == 0:
                continue
            yd = 3 - y if a else y
            group = 1 - pair if a else pair
            peers.append((xd * 4 + yd, a, xd, 2 * xd + group))

    def local(src, dst, sem):
        return pltpu.make_async_copy(src, dst, sem)

    def remote(src, dst, ssem, rsem, section, expert):
        return pltpu.make_async_remote_copy(
            src_ref=src,
            dst_ref=dst,
            send_sem=ssem,
            recv_sem=rsem,
            device_id=(section, expert),
            device_id_type=MESH,
        )

    loads = [
        local(left_in.at[0], tok.at[0], load_sem.at[0]),
        local(left_saved.at[0], tok.at[1], load_sem.at[1]),
        local(left_cot.at[0], tok.at[2], load_sem.at[2]),
        local(w_gate.at[0, 0], wgu.at[:, pl.ds(0, HALF)], load_sem.at[3]),
        local(w_up.at[0, 0], wgu.at[:, pl.ds(HALF, HALF)], load_sem.at[4]),
        local(w_down.at[0, 0], wd, load_sem.at[5]),
        local(left_new, tok.at[3], load_sem.at[6]),
        local(right_cot_new, tok.at[4], load_sem.at[7]),
    ]
    for copy in loads:
        copy.start()

    barrier = pltpu.get_barrier_semaphore()
    for dest, _, _, _ in peers:
        pl.semaphore_signal(barrier, inc=1, device_id=(sec, dest), device_id_type=MESH)
    pl.semaphore_signal(barrier, inc=1, device_id=(sec, partner), device_id_type=MESH)
    for other in (mirror, after, ahead):
        pl.semaphore_signal(barrier, inc=1, device_id=(other, me), device_id_type=MESH)

    eye = iota((TOK, TOK), 0) == iota((TOK, TOK), 1)
    upper = (iota((TOK, TOK), 0) < iota((TOK, TOK), 1)).astype(BF)

    def code_of(j):
        q = j % 8
        return (lax.div(j, 8) % 8) * 16 + jnp.where(j < 64, q, 8 + lax.div(q, 4))

    code_rows = code_of(iota((128, TOK), 0)).astype(F32)
    code_cols = code_of(iota((TOK, 128), 1)).astype(F32)
    for p in range(6):
        ids = ids_ref[p : p + 1, :]
        onehot = (ids == iota((8, TOK), 0)).astype(F32)
        before = dot(onehot.astype(BF), upper)
        rank = jnp.sum(before * onehot, axis=0, keepdims=True)
        target = ids.astype(F32) * 16.0 + rank
        ptab[p] = (code_rows == target).astype(F32).astype(BF)
        column = jnp.sum(jnp.where(eye, target, 0.0), axis=1, keepdims=True)
        pttab[p] = (code_cols == column).astype(F32).astype(BF)
        gate = jnp.sum(jnp.where(eye, gates_ref[p : p + 1, :], 0.0), axis=1, keepdims=True)
        gtab[p] = jnp.broadcast_to(gate, (TOK, 128))

    pl.semaphore_wait(barrier, 11)

    mirror_sources = [right_cot.at[0], right_saved.at[0, 0], right_in.at[0], right_saved.at[1, 0]]
    mirrors = [
        remote(src, mir.at[i], mir_sem.at[0, i], mir_sem.at[1, i], mirror, me)
        for i, src in enumerate(mirror_sources)
    ]
    for copy in mirrors:
        copy.start()

    quarter64 = iota((TOK, CHUNK), 0) % 4
    quarter128 = iota((128, CHUNK), 0) % 4

    def gather(unit, p, read, scaled):
        place = ptab[p]
        extra = None
        for c in range(4):
            cols = pl.ds(c * CHUNK, CHUNK)
            block = read(cols)
            if scaled:
                block = (gtab[p][:, 0:1] * block.astype(F32)).astype(BF)
            routed = dot(place, block)
            send[unit, :, :, cols] = routed[:64].reshape(8, 8, CHUNK).astype(BF)
            tail = routed[64:]
            extra = tail if c == 0 else jnp.where(quarter64 == c, tail, extra)
        send[unit, :, :, pl.ds(D, CHUNK)] = extra.reshape(8, 8, CHUNK).astype(BF)
        for dest, a, _, expert in peers:
            remote(
                send.at[unit, expert],
                recv.at[unit, 4 * a + x],
                s1_send.at[unit],
                s1_recv.at[unit, a],
                sec,
                dest,
            ).start()
        recv[unit, x] = send[unit, mine]

    def relay(unit):
        for a in (1, 0):
            count = 4 if a else 3
            span = recv.at[unit, pl.ds(4 * a, count)]
            remote(span, span, s1_send.at[unit], s1_recv.at[unit, a], sec, partner).wait_recv()
            remote(
                recv.at[unit, pl.ds(4 * a, 4)],
                recv.at[unit, pl.ds(8 + 4 * a, 4)],
                rl_send.at[unit, a],
                rl_recv.at[unit, a],
                sec,
                partner,
            ).start()

    def relayed(unit):
        for a in (1, 0):
            span = recv.at[unit, pl.ds(4 * a, 4)]
            remote(span, span, rl_send.at[unit, a], rl_recv.at[unit, a], sec, partner).wait_recv()

    pick_j = iota((32, 128), 1)
    pick_r = iota((32, 128), 0)
    spread = (lax.div(iota((128, 32), 0), 4) == iota((128, 32), 1)).astype(F32).astype(BF)

    def unfold(unit, dst, base):
        for c in range(4):
            cols = pl.ds(c * CHUNK, CHUNK)
            first = recv[unit, :, :, cols].astype(F32).reshape(128, CHUNK).astype(BF)
            dst[pl.ds(base, 128), cols] = first
        tail = recv[unit, :, :, pl.ds(D, CHUNK)].astype(F32).reshape(128, CHUNK).astype(BF)
        for c in range(4):
            pick = (pick_j == 4 * pick_r + c).astype(F32).astype(BF)
            dst[pl.ds(base + 128, 32), pl.ds(c * CHUNK, CHUNK)] = dot(pick, tail).astype(BF)

    def fold(r, chunk_of):
        extra = None
        for c in range(4):
            rows = chunk_of(c)
            part[r, :, :, pl.ds(c * CHUNK, CHUNK)] = (
                rows[:128].reshape(16, 8, CHUNK).astype(BF)
            )
            tail = dot(spread, rows[128:].astype(BF))
            extra = tail if c == 0 else jnp.where(quarter128 == c, tail, extra)
        part[r, :, :, pl.ds(D, CHUNK)] = extra.reshape(16, 8, CHUNK).astype(BF)
        remote(
            part.at[r, pl.ds(8, 8)], half.at[r], pt_send.at[r], pt_recv.at[r], sec, partner
        ).start()

    def gate_up(rows):
        return [dot(rows[...], wgu[:, pl.ds(256 * i, 256)]) for i in range(3)]

    def expert_forward(unit, r):
        relayed(unit)
        unfold(unit, xfwd, 0)
        both = jnp.concatenate(gate_up(xfwd), axis=1)
        gate, up = both[:, :HALF], both[:, HALF:]
        hidden = (gate * jax.nn.sigmoid(gate) * up).astype(BF)
        fold(r, lambda c: dot(hidden, wd[:, pl.ds(c * CHUNK, CHUNK)]))

    def expert_backward(unit_x, unit_c, index, r):
        base = index * ROWS
        rows = pl.ds(base, ROWS)
        relayed(unit_x)
        unfold(unit_x, xall, base)
        both = jnp.concatenate(gate_up(xall.at[rows]), axis=1)
        gate, up = both[:, :HALF], both[:, HALF:]
        logistic = jax.nn.sigmoid(gate)
        swish = gate * logistic
        hid[rows] = (swish * up).astype(BF)
        relayed(unit_c)
        unfold(unit_c, call, base)
        d_hidden = dot_nt(call[rows], wd[...])
        d_gate = (d_hidden * up * logistic * (1.0 + gate * (1.0 - logistic))).astype(BF)
        d_up = (d_hidden * swish).astype(BF)
        dgu[rows, pl.ds(0, HALF)] = d_gate
        dgu[rows, pl.ds(HALF, HALF)] = d_up
        fold(r, lambda c: dot_nt(dgu[rows], wgu[pl.ds(c * CHUNK, CHUNK), :]))

    def add_halves(r):
        remote(half.at[r], half.at[r], pt_send.at[r], pt_recv.at[r], sec, partner).wait_recv()
        for i in range(8):
            sums[r, i] = (part[r, i].astype(F32) + half[r, i].astype(F32)).astype(BF)
        for dest, a, xd, _ in peers:
            remote(
                sums.at[r, 4 * a + xd],
                vals.at[r, mine],
                sm_send.at[r],
                sm_recv.at[r],
                sec,
                dest,
            ).start()
        vals[r, mine] = sums[r, x]

    def combine(r, p, read, scaled, index):
        span = vals.at[r, pl.ds(0, 7)]
        remote(span, span, sm_send.at[r], sm_recv.at[r], sec, partner).wait_recv()
        back = pttab[p]
        tail = vals[r, :, :, pl.ds(D, CHUNK)].astype(F32).reshape(TOK, CHUNK)
        for c in range(4):
            cols = pl.ds(c * CHUNK, CHUNK)
            first = vals[r, :, :, cols].astype(F32).reshape(TOK, CHUNK)
            last = jnp.where(quarter64 == c, tail, 0.0)
            rows = jnp.concatenate([first, last], axis=0).astype(BF)
            got = dot(back, rows)
            if scaled:
                got = gtab[p][:, 0:1] * got
            outs[index, :, cols] = (read(cols).astype(F32) + got).astype(BF)

    def from_tok(i):
        return lambda cols: tok[i, :, cols]

    def from_mir(i):
        return lambda cols: mir[i, :, cols]

    def choose(edge, i, j):
        return lambda cols: jnp.where(
            sec == edge, tok[i, :, cols].astype(F32), passed[j, :, cols].astype(F32)
        ).astype(BF)

    left_two = choose(0, 3, 0)
    cot_two = choose(15, 4, 1)
    pass_left = remote(outs.at[0], passed.at[0], ps_sem.at[0, 0], ps_sem.at[1, 0], after, me)
    pass_right = remote(outs.at[1], passed.at[1], ps_sem.at[0, 1], ps_sem.at[1, 1], ahead, me)
    out_copies = [
        local(outs.at[0], left_out.at[0], out_sem.at[0]),
        local(outs.at[1], right_back.at[0], out_sem.at[1]),
        local(outs.at[2], right_out, out_sem.at[2]),
        local(outs.at[3], left_back, out_sem.at[3]),
        local(outs.at[4], left_out.at[1], out_sem.at[4]),
        local(outs.at[5], right_back.at[1], out_sem.at[5]),
        local(gg_buf, grad_gate, out_sem.at[6]),
        local(gu_buf, grad_up, out_sem.at[7]),
        local(gd_buf, grad_down, out_sem.at[8]),
    ]

    R_F0, R_B0, R_F1, R_B1, R_F2, R_B2 = range(6)
    loads[0].wait()
    gather(U_F0, F0, from_tok(0), False)
    loads[1].wait()
    gather(U_B1X, B1, from_tok(1), False)
    loads[2].wait()
    relay(U_F0)
    gather(U_B1C, B1, from_tok(2), True)
    relay(U_B1X)
    relay(U_B1C)
    for copy in loads[3:]:
        copy.wait()
    expert_forward(U_F0, R_F0)
    mirrors[0].wait_recv()
    gather(U_B0C, B0, from_mir(0), True)
    mirrors[1].wait_recv()
    gather(U_B0X, B0, from_mir(1), False)
    relay(U_B0C)
    relay(U_B0X)
    expert_backward(U_B1X, U_B1C, 0, R_B1)
    add_halves(R_F0)
    combine(R_F0, F0, from_tok(0), True, 0)
    pass_left.start()
    out_copies[0].start()
    pass_left.wait_recv()
    gather(U_F2, F2, left_two, False)
    relay(U_F2)
    expert_backward(U_B0X, U_B0C, 1, R_B0)
    add_halves(R_B1)
    combine(R_B1, B1, from_tok(2), False, 3)
    out_copies[3].start()
    mirrors[2].wait_recv()
    gather(U_F1, F1, from_mir(2), False)
    mirrors[3].wait_recv()
    gather(U_B2X, B2, from_mir(3), False)
    relay(U_F1)
    relay(U_B2X)
    expert_forward(U_F2, R_F2)
    add_halves(R_B0)
    combine(R_B0, B0, from_mir(0), False, 1)
    pass_right.start()
    out_copies[1].start()
    pass_right.wait_recv()
    gather(U_B2C, B2, cot_two, True)
    relay(U_B2C)
    expert_forward(U_F1, R_F1)
    add_halves(R_F2)
    combine(R_F2, F2, left_two, True, 4)
    out_copies[4].start()
    expert_backward(U_B2X, U_B2C, 2, R_B2)
    add_halves(R_F1)
    combine(R_F1, F1, from_mir(2), True, 2)
    out_copies[2].start()

    def grads_of_inputs(i, carry):
        cols = pl.ds(pl.multiple_of(i * 256, 256), 256)
        total = dot_tn(xall[:, cols], dgu[...]).astype(BF)
        gg_buf[cols, :] = total[:, :HALF]
        gu_buf[cols, :] = total[:, HALF:]
        return carry

    def grads_of_down(i, carry):
        cols = pl.ds(pl.multiple_of(i * 256, 256), 256)
        gd_buf[:, cols] = dot_tn(hid[...], call[:, cols]).astype(BF)
        return carry

    lax.fori_loop(0, 8, grads_of_inputs, 0)
    out_copies[6].start()
    out_copies[7].start()
    add_halves(R_B2)
    lax.fori_loop(0, 8, grads_of_down, 0)
    out_copies[8].start()
    combine(R_B2, B2, cot_two, False, 5)
    out_copies[5].start()

    for copy in mirrors:
        copy.wait_send()
    pass_left.wait_send()
    pass_right.wait_send()
    for unit in range(9):
        span = send.at[unit, pl.ds(0, 7)]
        remote(span, span, s1_send.at[unit], s1_recv.at[unit, 0], sec, partner).wait_send()
        for a in range(2):
            span = recv.at[unit, pl.ds(4 * a, 4)]
            remote(span, span, rl_send.at[unit, a], rl_recv.at[unit, a], sec, partner).wait_send()
    for r in range(6):
        span = part.at[r, pl.ds(8, 8)]
        remote(span, span, pt_send.at[r], pt_recv.at[r], sec, partner).wait_send()
        span = sums.at[r, pl.ds(0, 7)]
        remote(span, span, sm_send.at[r], sm_recv.at[r], sec, partner).wait_send()
    for copy in out_copies:
        copy.wait()


def per_device(
    left_in,
    left_new,
    left_saved,
    left_cot,
    right_in,
    right_saved,
    right_cot,
    right_cot_new,
    expert_ids,
    gate_values,
    w_gate,
    w_up,
    w_down,
):
    ids = expert_ids.reshape(6, TOK)
    gates = gate_values.reshape(6, TOK)
    anywhere = pl.BlockSpec(memory_space=pl.ANY)
    vmem = pl.BlockSpec(memory_space=pltpu.VMEM)
    sds = jax.ShapeDtypeStruct
    dma = pltpu.SemaphoreType.DMA
    outs = pl.pallas_call(
        kernel,
        name="relay",
        out_shape=(
            sds((2, TOK, D), BF),
            sds((TOK, D), BF),
            sds((TOK, D), BF),
            sds((2, TOK, D), BF),
            sds((D, HALF), BF),
            sds((D, HALF), BF),
            sds((HALF, D), BF),
        ),
        in_specs=[vmem, vmem] + [anywhere] * 11,
        out_specs=(anywhere,) * 7,
        scratch_shapes=[
            pltpu.VMEM((6, 128, TOK), BF),
            pltpu.VMEM((6, TOK, 128), BF),
            pltpu.VMEM((6, TOK, 128), F32),
            pltpu.VMEM((D, 2 * HALF), BF),
            pltpu.VMEM((HALF, D), BF),
            pltpu.VMEM((5, TOK, D), BF),
            pltpu.VMEM((4, TOK, D), BF),
            pltpu.VMEM((2, TOK, D), BF),
            pltpu.VMEM((6, TOK, D), BF),
            pltpu.VMEM((9, 8, 8, SLAB), BF),
            pltpu.VMEM((9, 16, 8, SLAB), BF),
            pltpu.VMEM((6, 16, 8, SLAB), BF),
            pltpu.VMEM((6, 8, 8, SLAB), BF),
            pltpu.VMEM((6, 8, 8, SLAB), BF),
            pltpu.VMEM((6, 8, 8, SLAB), BF),
            pltpu.VMEM((3 * ROWS, D), BF),
            pltpu.VMEM((3 * ROWS, D), BF),
            pltpu.VMEM((3 * ROWS, 2 * HALF), BF),
            pltpu.VMEM((3 * ROWS, HALF), BF),
            pltpu.VMEM((ROWS, D), BF),
            pltpu.VMEM((D, HALF), BF),
            pltpu.VMEM((D, HALF), BF),
            pltpu.VMEM((HALF, D), BF),
            dma((8,)),
            dma((2, 4)),
            dma((9,)),
            dma((9, 2)),
            dma((9, 2)),
            dma((9, 2)),
            dma((6,)),
            dma((6,)),
            dma((6,)),
            dma((6,)),
            dma((2, 2)),
            dma((9,)),
        ],
        compiler_params=pltpu.CompilerParams(
            collective_id=0, has_side_effects=True, vmem_limit_bytes=62 * 1024 * 1024
        ),
    )(
        ids,
        gates,
        left_in,
        left_new,
        left_saved,
        left_cot,
        right_in,
        right_saved,
        right_cot,
        right_cot_new,
        w_gate,
        w_up,
        w_down,
    )
    left_out, right_out, left_back, right_back, gg, gu, gd = outs
    return (
        left_out[:, None],
        right_out[None],
        left_back[None],
        right_back[:, None],
        gg[None, None],
        gu[None, None],
        gd[None, None],
    )


def solution(mesh):
    in_specs = (
        P("section", "expert", None),
        P("expert", None),
        P("section", "expert", None),
        P("section", "expert", None),
        P("section", "expert", None),
        P(None, "section", "expert", None),
        P("section", "expert", None),
        P("expert", None),
        P(None, None, "section", "expert", None),
        P(None, None, "section", "expert", None),
        P("section", "expert", None, None),
        P("section", "expert", None, None),
        P("section", "expert", None, None),
    )
    out_specs = (
        P(None, "section", "expert", None),
        P("section", "expert", None),
        P("section", "expert", None),
        P(None, "section", "expert", None),
        P("section", "expert", None, None),
        P("section", "expert", None, None),
        P("section", "expert", None, None),
    )
    return jax.shard_map(
        per_device, mesh=mesh, in_specs=in_specs, out_specs=out_specs, check_vma=False
    )
```

profile of v0, /device:TPU:9, one launch (start us, length us, event | category | flops | bytes accessed | tf_op | source)
XLA Modules:
  0.0 153.3 jit_solution(1164994428016305770)
XLA Ops:
  0.6 0.5 broadcast.6
  1.1 1.3 reduce.6
  2.5 0.6 reshape.20.ids_ref
  3.1 0.5 broadcast.7
  3.6 1.3 reduce.7
  5.0 0.6 reshape.21.gates_ref
  5.6 137.4 %relay.1 = (bf16[2,64,2048]{2,1,0:T(8,128)(2,1)}, bf16[64,2048]{1,0:T(8,128)(2,1)}, bf16[64,2048]{1,0:T(8,128)(2,1)}, bf16[2,64,2048]{2,1,0:T(8,128)(2,1)}, bf16...) custom-call(s32[6,64]{1,0:T(8,128)} %reshape.20.ids_ref, f32[6,64]{1,0:T(8,128)} %reshape.21.gates_ref, ...), custom_call_target="tpu_custom_call" | custom-call | tf_op jit(solution)/shard_map/relay/pallas_call | solution.py:456
  143.0 0.0 copy-start.4
  143.0 0.0 copy-start.3
  143.0 0.0 copy-start.2
  143.0 2.0 %copy.37 = bf16[2,1,64,2048]{3,2,1,0:T(8,128)(2,1)} copy(bf16[2,1,64,2048]{3,2,1,0:T(8,128)(2,1)} %bitcast.19) | data formatting | bytes 1048576
  145.0 1.7 %copy.38 = bf16[1,64,2048]{2,1,0:T(8,128)(2,1)} copy(bf16[1,64,2048]{2,1,0:T(8,128)(2,1)} %bitcast.21) | data formatting | bytes 524288
  146.7 0.0 copy-done.4
  146.7 0.7 copy.39
  147.4 0.0 copy-done.3
  147.4 0.8 copy.40
  148.2 0.0 copy-done.2
  148.2 0.0 copy-start.1
  148.2 1.1 copy.41
  149.3 0.8 copy-done.1
  150.2 0.0 copy-start
  150.2 1.1 copy.42
  151.3 0.8 copy-done
  152.2 1.1 copy.43
Async XLA Ops:
  143.0 3.7 %copy-start.4 = (bf16[64,2048]{1,0:T(8,128)(2,1)S(1)}, bf16[64,2048]{1,0:T(8,128)(2,1)}, u32[]{:S(2)}) copy-start(bf16[64,2048]{1,0:T(8,128)(2,1)} %get-tuple-element.16) | copy-start | bytes 786436
  143.0 4.4 %copy-start.3 = (bf16[2,64,2048]{2,1,0:T(8,128)(2,1)S(1)}, bf16[2,64,2048]{2,1,0:T(8,128)(2,1)}, u32[]{:S(2)}) copy-start(bf16[2,64,2048]{2,1,0:T(8,128)(2,1)} %get-tuple-element.17) | copy-start | bytes 1572868
  143.0 5.2 %copy-start.2 = (bf16[2048,384]{1,0:T(8,128)(2,1)S(1)}, bf16[2048,384]{1,0:T(8,128)(2,1)}, u32[]{:S(2)}) copy-start(bf16[2048,384]{1,0:T(8,128)(2,1)} %get-tuple-element.18) | copy-start | bytes 4718596
  148.2 2.0 %copy-start.1 = (bf16[2048,384]{1,0:T(8,128)(2,1)S(1)}, bf16[2048,384]{1,0:T(8,128)(2,1)}, u32[]{:S(2)}) copy-start(bf16[2048,384]{1,0:T(8,128)(2,1)} %get-tuple-element.19) | copy-start | bytes 4718596
  150.2 2.0 %copy-start = (bf16[384,2048]{1,0:T(8,128)(2,1)S(1)}, bf16[384,2048]{1,0:T(8,128)(2,1)}, u32[]{:S(2)}) copy-start(bf16[384,2048]{1,0:T(8,128)(2,1)} %get-tuple-element.20) | copy-start | bytes 4718596
where the time goes:
time: 154 us; the launch traced here: 153 us
  Pallas kernels  137 us (89%)
  local copies, waits for them, and re-layouts  12.5 us (8%)
  other arithmetic  2.7 us (2%)
    pallas_call x1, Pallas kernels, per_device(): pl.pallas_call(kernel, name='relay', out_shape=(sds((2, TOK, D), BF), sds...  137 us
    unnamed x19, local copies, waits for them, and re-layouts  11.3 us

commit v1 on v0

--- a/solution.py
+++ b/solution.py
@@ -36,8 +36,8 @@
 
 
 def kernel(
-    ids_ref,
-    gates_ref,
+    ids_hbm,
+    gates_hbm,
     left_in,
     left_new,
     left_saved,
@@ -49,13 +49,12 @@
     w_gate,
     w_up,
     w_down,
-    left_out,
-    right_out,
-    left_back,
-    right_back,
-    grad_gate,
-    grad_up,
-    grad_down,
+    outs,
+    gg_buf,
+    gu_buf,
+    gd_buf,
+    ids_ref,
+    gates_ref,
     ptab,
     pttab,
     gtab,
@@ -64,7 +63,6 @@
     tok,
     mir,
     passed,
-    outs,
     send,
     recv,
     part,
@@ -76,9 +74,6 @@
     dgu,
     hid,
     xfwd,
-    gg_buf,
-    gu_buf,
-    gd_buf,
     load_sem,
     mir_sem,
     s1_send,
@@ -90,7 +85,6 @@
     sm_send,
     sm_recv,
     ps_sem,
-    out_sem,
 ):
     sec = lax.axis_index("section")
     me = lax.axis_index("expert")
@@ -126,6 +120,10 @@
             device_id_type=MESH,
         )
 
+    id_loads = [
+        local(ids_hbm, ids_ref, load_sem.at[8]),
+        local(gates_hbm, gates_ref, load_sem.at[9]),
+    ]
     loads = [
         local(left_in.at[0], tok.at[0], load_sem.at[0]),
         local(left_saved.at[0], tok.at[1], load_sem.at[1]),
@@ -136,7 +134,7 @@
         local(left_new, tok.at[3], load_sem.at[6]),
         local(right_cot_new, tok.at[4], load_sem.at[7]),
     ]
-    for copy in loads:
+    for copy in id_loads + loads:
         copy.start()
 
     barrier = pltpu.get_barrier_semaphore()
@@ -155,8 +153,10 @@
 
     code_rows = code_of(iota((128, TOK), 0)).astype(F32)
     code_cols = code_of(iota((TOK, 128), 1)).astype(F32)
+    for copy in id_loads:
+        copy.wait()
     for p in range(6):
-        ids = ids_ref[p : p + 1, :]
+        ids = ids_ref[p // 2, p % 2, 0]
         onehot = (ids == iota((8, TOK), 0)).astype(F32)
         before = dot(onehot.astype(BF), upper)
         rank = jnp.sum(before * onehot, axis=0, keepdims=True)
@@ -164,18 +164,14 @@
         ptab[p] = (code_rows == target).astype(F32).astype(BF)
         column = jnp.sum(jnp.where(eye, target, 0.0), axis=1, keepdims=True)
         pttab[p] = (code_cols == column).astype(F32).astype(BF)
-        gate = jnp.sum(jnp.where(eye, gates_ref[p : p + 1, :], 0.0), axis=1, keepdims=True)
+        gate = jnp.sum(jnp.where(eye, gates_ref[p // 2, p % 2, 0], 0.0), axis=1, keepdims=True)
         gtab[p] = jnp.broadcast_to(gate, (TOK, 128))
-
-    pl.semaphore_wait(barrier, 11)
 
     mirror_sources = [right_cot.at[0], right_saved.at[0, 0], right_in.at[0], right_saved.at[1, 0]]
     mirrors = [
         remote(src, mir.at[i], mir_sem.at[0, i], mir_sem.at[1, i], mirror, me)
         for i, src in enumerate(mirror_sources)
     ]
-    for copy in mirrors:
-        copy.start()
 
     quarter64 = iota((TOK, CHUNK), 0) % 4
     quarter128 = iota((128, CHUNK), 0) % 4
@@ -193,6 +189,9 @@
             tail = routed[64:]
             extra = tail if c == 0 else jnp.where(quarter64 == c, tail, extra)
         send[unit, :, :, pl.ds(D, CHUNK)] = extra.reshape(8, 8, CHUNK).astype(BF)
+        recv[unit, x] = send[unit, mine]
+
+    def ship(unit):
         for dest, a, _, expert in peers:
             remote(
                 send.at[unit, expert],
@@ -202,7 +201,6 @@
                 sec,
                 dest,
             ).start()
-        recv[unit, x] = send[unit, mine]
 
     def relay(unit):
         for a in (1, 0):
@@ -326,26 +324,21 @@
     cot_two = choose(15, 4, 1)
     pass_left = remote(outs.at[0], passed.at[0], ps_sem.at[0, 0], ps_sem.at[1, 0], after, me)
     pass_right = remote(outs.at[1], passed.at[1], ps_sem.at[0, 1], ps_sem.at[1, 1], ahead, me)
-    out_copies = [
-        local(outs.at[0], left_out.at[0], out_sem.at[0]),
-        local(outs.at[1], right_back.at[0], out_sem.at[1]),
-        local(outs.at[2], right_out, out_sem.at[2]),
-        local(outs.at[3], left_back, out_sem.at[3]),
-        local(outs.at[4], left_out.at[1], out_sem.at[4]),
-        local(outs.at[5], right_back.at[1], out_sem.at[5]),
-        local(gg_buf, grad_gate, out_sem.at[6]),
-        local(gu_buf, grad_up, out_sem.at[7]),
-        local(gd_buf, grad_down, out_sem.at[8]),
-    ]
-
     R_F0, R_B0, R_F1, R_B1, R_F2, R_B2 = range(6)
     loads[0].wait()
     gather(U_F0, F0, from_tok(0), False)
     loads[1].wait()
     gather(U_B1X, B1, from_tok(1), False)
     loads[2].wait()
+    gather(U_B1C, B1, from_tok(2), True)
+
+    pl.semaphore_wait(barrier, 11)
+    for copy in mirrors:
+        copy.start()
+    ship(U_F0)
+    ship(U_B1X)
+    ship(U_B1C)
     relay(U_F0)
-    gather(U_B1C, B1, from_tok(2), True)
     relay(U_B1X)
     relay(U_B1C)
     for copy in loads[3:]:
@@ -353,44 +346,45 @@
     expert_forward(U_F0, R_F0)
     mirrors[0].wait_recv()
     gather(U_B0C, B0, from_mir(0), True)
+    ship(U_B0C)
     mirrors[1].wait_recv()
     gather(U_B0X, B0, from_mir(1), False)
+    ship(U_B0X)
     relay(U_B0C)
     relay(U_B0X)
     expert_backward(U_B1X, U_B1C, 0, R_B1)
     add_halves(R_F0)
     combine(R_F0, F0, from_tok(0), True, 0)
     pass_left.start()
-    out_copies[0].start()
     pass_left.wait_recv()
     gather(U_F2, F2, left_two, False)
+    ship(U_F2)
     relay(U_F2)
     expert_backward(U_B0X, U_B0C, 1, R_B0)
     add_halves(R_B1)
     combine(R_B1, B1, from_tok(2), False, 3)
-    out_copies[3].start()
     mirrors[2].wait_recv()
     gather(U_F1, F1, from_mir(2), False)
+    ship(U_F1)
     mirrors[3].wait_recv()
     gather(U_B2X, B2, from_mir(3), False)
+    ship(U_B2X)
     relay(U_F1)
     relay(U_B2X)
     expert_forward(U_F2, R_F2)
     add_halves(R_B0)
     combine(R_B0, B0, from_mir(0), False, 1)
     pass_right.start()
-    out_copies[1].start()
     pass_right.wait_recv()
     gather(U_B2C, B2, cot_two, True)
+    ship(U_B2C)
     relay(U_B2C)
     expert_forward(U_F1, R_F1)
     add_halves(R_F2)
     combine(R_F2, F2, left_two, True, 4)
-    out_copies[4].start()
     expert_backward(U_B2X, U_B2C, 2, R_B2)
     add_halves(R_F1)
     combine(R_F1, F1, from_mir(2), True, 2)
-    out_copies[2].start()
 
     def grads_of_inputs(i, carry):
         cols = pl.ds(pl.multiple_of(i * 256, 256), 256)
@@ -405,13 +399,9 @@
         return carry
 
     lax.fori_loop(0, 8, grads_of_inputs, 0)
-    out_copies[6].start()
-    out_copies[7].start()
     add_halves(R_B2)
     lax.fori_loop(0, 8, grads_of_down, 0)
-    out_copies[8].start()
     combine(R_B2, B2, cot_two, False, 5)
-    out_copies[5].start()
 
     for copy in mirrors:
         copy.wait_send()
@@ -428,7 +418,37 @@
         remote(span, span, pt_send.at[r], pt_recv.at[r], sec, partner).wait_send()
         span = sums.at[r, pl.ds(0, 7)]
         remote(span, span, sm_send.at[r], sm_recv.at[r], sec, partner).wait_send()
-    for copy in out_copies:
+
+
+def write_out(
+    outs,
+    gg_buf,
+    gu_buf,
+    gd_buf,
+    left_out,
+    right_out,
+    left_back,
+    right_back,
+    grad_gate,
+    grad_up,
+    grad_down,
+    sem,
+):
+    pairs = [
+        (gg_buf, grad_gate),
+        (gu_buf, grad_up),
+        (gd_buf, grad_down),
+        (outs.at[0], left_out.at[0]),
+        (outs.at[1], right_back.at[0]),
+        (outs.at[2], right_out),
+        (outs.at[3], left_back),
+        (outs.at[4], left_out.at[1]),
+        (outs.at[5], right_back.at[1]),
+    ]
+    copies = [pltpu.make_async_copy(a, b, sem.at[i]) for i, (a, b) in enumerate(pairs)]
+    for copy in copies:
+        copy.start()
+    for copy in copies:
         copy.wait()
 
 
@@ -447,27 +467,26 @@
     w_up,
     w_down,
 ):
-    ids = expert_ids.reshape(6, TOK)
-    gates = gate_values.reshape(6, TOK)
-    anywhere = pl.BlockSpec(memory_space=pl.ANY)
+    ids = jnp.swapaxes(expert_ids, 3, 4)
+    gates = jnp.swapaxes(gate_values, 3, 4)
+    hbm = pl.BlockSpec(memory_space=pltpu.HBM)
     vmem = pl.BlockSpec(memory_space=pltpu.VMEM)
     sds = jax.ShapeDtypeStruct
     dma = pltpu.SemaphoreType.DMA
-    outs = pl.pallas_call(
+    results = pl.pallas_call(
         kernel,
         name="relay",
         out_shape=(
-            sds((2, TOK, D), BF),
-            sds((TOK, D), BF),
-            sds((TOK, D), BF),
-            sds((2, TOK, D), BF),
-            sds((D, HALF), BF),
-            sds((D, HALF), BF),
-            sds((HALF, D), BF),
+            pltpu.VMEM((6, TOK, D), BF),
+            pltpu.VMEM((D, HALF), BF),
+            pltpu.VMEM((D, HALF), BF),
+            pltpu.VMEM((HALF, D), BF),
         ),
-        in_specs=[vmem, vmem] + [anywhere] * 11,
-        out_specs=(anywhere,) * 7,
+        in_specs=[hbm] * 13,
+        out_specs=(vmem,) * 4,
         scratch_shapes=[
+            pltpu.VMEM((3, 2, 1, 1, TOK), jnp.int32),
+            pltpu.VMEM((3, 2, 1, 1, TOK), F32),
             pltpu.VMEM((6, 128, TOK), BF),
             pltpu.VMEM((6, TOK, 128), BF),
             pltpu.VMEM((6, TOK, 128), F32),
@@ -476,7 +495,6 @@
             pltpu.VMEM((5, TOK, D), BF),
             pltpu.VMEM((4, TOK, D), BF),
             pltpu.VMEM((2, TOK, D), BF),
-            pltpu.VMEM((6, TOK, D), BF),
             pltpu.VMEM((9, 8, 8, SLAB), BF),
             pltpu.VMEM((9, 16, 8, SLAB), BF),
             pltpu.VMEM((6, 16, 8, SLAB), BF),
@@ -488,10 +506,7 @@
             pltpu.VMEM((3 * ROWS, 2 * HALF), BF),
             pltpu.VMEM((3 * ROWS, HALF), BF),
             pltpu.VMEM((ROWS, D), BF),
-            pltpu.VMEM((D, HALF), BF),
-            pltpu.VMEM((D, HALF), BF),
-            pltpu.VMEM((HALF, D), BF),
-            dma((8,)),
+            dma((10,)),
             dma((2, 4)),
             dma((9,)),
             dma((9, 2)),
@@ -502,10 +517,9 @@
             dma((6,)),
             dma((6,)),
             dma((2, 2)),
-            dma((9,)),
         ],
         compiler_params=pltpu.CompilerParams(
-            collective_id=0, has_side_effects=True, vmem_limit_bytes=62 * 1024 * 1024
+            collective_id=0, has_side_effects=True, vmem_limit_bytes=60700000
         ),
     )(
         ids,
@@ -522,7 +536,23 @@
         w_up,
         w_down,
     )
-    left_out, right_out, left_back, right_back, gg, gu, gd = outs
+    left_out, right_out, left_back, right_back, gg, gu, gd = pl.pallas_call(
+        write_out,
+        name="write_out",
+        out_shape=(
+            sds((2, TOK, D), BF),
+            sds((TOK, D), BF),
+            sds((TOK, D), BF),
+            sds((2, TOK, D), BF),
+            sds((D, HALF), BF),
+            sds((D, HALF), BF),
+            sds((HALF, D), BF),
+        ),
+        in_specs=[vmem] * 4,
+        out_specs=(hbm,) * 7,
+        scratch_shapes=[dma((9,))],
+        compiler_params=pltpu.CompilerParams(vmem_limit_bytes=4 * 1024 * 1024),
+    )(*results)
     return (
         left_out[:, None],
         right_out[None],

time: 154 us -> 140 us (0.909)
  local copies, waits for them, and re-layouts: 12.5 us -> 0 us
  other arithmetic: 2.7 us -> 0 us
  Pallas kernels: 137 us -> 139 us
    unnamed x19 -> x0, local copies, waits for them, and re-layouts: 11.3 us -> none
    unnamed x2 -> x0, other arithmetic: 2.7 us -> none
    pallas_call x1 -> x2, Pallas kernels: 137 us -> 139 us  [the longest x1 136 us: per_device(): pl.pallas_call(kernel, name='relay', out_shape=(pltpu.VMEM((6, TOK, D), B...]
where the time goes in v1:
time: 140 us
  Pallas kernels  139 us (99%)
    pallas_call x1, Pallas kernels, per_device(): pl.pallas_call(kernel, name='relay', out_shape=(pltpu.VMEM((6, TOK, D), B...  136 us

profile of v1, /device:TPU:9, one launch (start us, length us, event | category | flops | bytes accessed | tf_op | source)
XLA Modules:
  0.0 139.6 jit_solution(9919082934115725492)
XLA Ops:
  0.6 136.1 %relay.1 = (bf16[6,64,2048]{2,1,0:T(8,128)(2,1)S(1)}, bf16[2048,384]{1,0:T(8,128)(2,1)S(1)}, bf16[2048,384]{1,0:T(8,128)(2,1)S(1)}, bf16[384,2048]{1,0:T(8,128)(2,1)S(1)}) custom-call(s32[3,2,1,1,64]{4,3,2,1,0:T(1,128)} %bitcast.13, f32[3,2,1,1,64]{4,3,2,1,0:T(1,128)} %bitcast.14, bf16[1,64,2048]{2,1,0:T(8,128)(2,1)} %left_in.1, bf16[64,2048]{1,0:T(8,128)(2,1)} %left_new.1, ...), custom_call_target="tpu_custom_call" | custom-call | tf_op jit(solution)/shard_map/relay/pallas_call | solution.py:476
  136.7 2.7 %write_out.1 = (bf16[2,64,2048]{2,1,0:T(8,128)(2,1)}, bf16[64,2048]{1,0:T(8,128)(2,1)}, bf16[64,2048]{1,0:T(8,128)(2,1)}, bf16[2,64,2048]{2,1,0:T(8,128)(2,1)}, ...) custom-call(bf16[6,64,2048]{2,1,0:T(8,128)(2,1)S(1)} %get-tuple-element.18.outs, ...), custom_call_target="tpu_custom_call" | custom-call | tf_op jit(solution)/shard_map/write_out/pallas_call | solution.py:539

commit v2 on v1

--- a/solution.py
+++ b/solution.py
@@ -55,6 +55,9 @@
     gd_buf,
     ids_ref,
     gates_ref,
+    partner_ids,
+    gathered,
+    swapped,
     ptab,
     pttab,
     gtab,
@@ -85,6 +88,8 @@
     sm_send,
     sm_recv,
     ps_sem,
+    id_sem,
+    gt_sem,
 ):
     sec = lax.axis_index("section")
     me = lax.axis_index("expert")
@@ -155,19 +160,26 @@
     code_cols = code_of(iota((TOK, 128), 1)).astype(F32)
     for copy in id_loads:
         copy.wait()
-    for p in range(6):
-        ids = ids_ref[p // 2, p % 2, 0]
+
+    def targets(ids):
         onehot = (ids == iota((8, TOK), 0)).astype(F32)
         before = dot(onehot.astype(BF), upper)
         rank = jnp.sum(before * onehot, axis=0, keepdims=True)
-        target = ids.astype(F32) * 16.0 + rank
+        return ids.astype(F32) * 16.0 + rank
+
+    def way_back(target):
+        column = jnp.sum(jnp.where(eye, target, 0.0), axis=1, keepdims=True)
+        return (code_cols == column).astype(F32).astype(BF)
+
+    for p in range(6):
+        target = targets(ids_ref[p // 2, p % 2, 0])
         ptab[p] = (code_rows == target).astype(F32).astype(BF)
-        column = jnp.sum(jnp.where(eye, target, 0.0), axis=1, keepdims=True)
-        pttab[p] = (code_cols == column).astype(F32).astype(BF)
+        pttab[p] = way_back(target)
         gate = jnp.sum(jnp.where(eye, gates_ref[p // 2, p % 2, 0], 0.0), axis=1, keepdims=True)
         gtab[p] = jnp.broadcast_to(gate, (TOK, 128))
 
     mirror_sources = [right_cot.at[0], right_saved.at[0, 0], right_in.at[0], right_saved.at[1, 0]]
+    id_swap = remote(ids_ref, partner_ids, id_sem.at[0], id_sem.at[1], sec, partner)
     mirrors = [
         remote(src, mir.at[i], mir_sem.at[0, i], mir_sem.at[1, i], mirror, me)
         for i, src in enumerate(mirror_sources)
@@ -245,20 +257,51 @@
             tail = dot(spread, rows[128:].astype(BF))
             extra = tail if c == 0 else jnp.where(quarter128 == c, tail, extra)
         part[r, :, :, pl.ds(D, CHUNK)] = extra.reshape(16, 8, CHUNK).astype(BF)
-        remote(
-            part.at[r, pl.ds(8, 8)], half.at[r], pt_send.at[r], pt_recv.at[r], sec, partner
-        ).start()
+
+    def hand_over(r):
+        for a in (1, 0):
+            remote(
+                part.at[r, pl.ds(8 + 4 * a, 4)],
+                half.at[r, pl.ds(4 * a, 4)],
+                pt_send.at[r, a],
+                pt_recv.at[r, a],
+                sec,
+                partner,
+            ).start()
+
+    def hand_out(r):
+        for dest, a, xd, _ in peers:
+            remote(
+                part.at[r, 8 + 4 * a + xd],
+                half.at[r, mine],
+                pt_send.at[r, 0],
+                pt_recv.at[r, 0],
+                sec,
+                dest,
+            ).start()
+        for dest, a, xd, _ in peers:
+            remote(
+                part.at[r, 4 * a + xd],
+                vals.at[r, mine],
+                sm_send.at[r],
+                sm_recv.at[r],
+                sec,
+                dest,
+            ).start()
+        half[r, mine] = part[r, 8 + x]
+        vals[r, mine] = part[r, x]
 
     def gate_up(rows):
         return [dot(rows[...], wgu[:, pl.ds(256 * i, 256)]) for i in range(3)]
 
-    def expert_forward(unit, r):
+    def expert_forward(unit, r, give):
         relayed(unit)
         unfold(unit, xfwd, 0)
         both = jnp.concatenate(gate_up(xfwd), axis=1)
         gate, up = both[:, :HALF], both[:, HALF:]
         hidden = (gate * jax.nn.sigmoid(gate) * up).astype(BF)
         fold(r, lambda c: dot(hidden, wd[:, pl.ds(c * CHUNK, CHUNK)]))
+        give(r)
 
     def expert_backward(unit_x, unit_c, index, r):
         base = index * ROWS
@@ -278,35 +321,63 @@
         dgu[rows, pl.ds(0, HALF)] = d_gate
         dgu[rows, pl.ds(HALF, HALF)] = d_up
         fold(r, lambda c: dot_nt(dgu[rows], wgu[pl.ds(c * CHUNK, CHUNK), :]))
+        hand_over(r)
 
     def add_halves(r):
-        remote(half.at[r], half.at[r], pt_send.at[r], pt_recv.at[r], sec, partner).wait_recv()
-        for i in range(8):
-            sums[r, i] = (part[r, i].astype(F32) + half[r, i].astype(F32)).astype(BF)
-        for dest, a, xd, _ in peers:
-            remote(
-                sums.at[r, 4 * a + xd],
-                vals.at[r, mine],
-                sm_send.at[r],
-                sm_recv.at[r],
-                sec,
-                dest,
-            ).start()
+        for a in (1, 0):
+            span = half.at[r, pl.ds(4 * a, 4)]
+            remote(span, span, pt_send.at[r, a], pt_recv.at[r, a], sec, partner).wait_recv()
+            for i in range(4 * a, 4 * a + 4):
+                sums[r, i] = (part[r, i].astype(F32) + half[r, i].astype(F32)).astype(BF)
+            for dest, side, xd, _ in peers:
+                if side == a:
+                    remote(
+                        sums.at[r, 4 * a + xd],
+                        vals.at[r, mine],
+                        sm_send.at[r],
+                        sm_recv.at[r],
+                        sec,
+                        dest,
+                    ).start()
         vals[r, mine] = sums[r, x]
 
-    def combine(r, p, read, scaled, index):
+    def rows_back(slabs, back, c):
+        first = slabs[:, :, pl.ds(c * CHUNK, CHUNK)].astype(F32).reshape(TOK, CHUNK)
+        tail = slabs[:, :, pl.ds(D, CHUNK)].astype(F32).reshape(TOK, CHUNK)
+        last = jnp.where(quarter64 == c, tail, 0.0)
+        return dot(back, jnp.concatenate([first, last], axis=0).astype(BF))
+
+    def arrived(r):
         span = vals.at[r, pl.ds(0, 7)]
         remote(span, span, sm_send.at[r], sm_recv.at[r], sec, partner).wait_recv()
-        back = pttab[p]
-        tail = vals[r, :, :, pl.ds(D, CHUNK)].astype(F32).reshape(TOK, CHUNK)
+
+    def combine(r, p, read, scaled, index):
+        arrived(r)
         for c in range(4):
             cols = pl.ds(c * CHUNK, CHUNK)
-            first = vals[r, :, :, cols].astype(F32).reshape(TOK, CHUNK)
-            last = jnp.where(quarter64 == c, tail, 0.0)
-            rows = jnp.concatenate([first, last], axis=0).astype(BF)
-            got = dot(back, rows)
+            got = rows_back(vals.at[r], pttab[p], c)
             if scaled:
                 got = gtab[p][:, 0:1] * got
+            outs[index, :, cols] = (read(cols).astype(F32) + got).astype(BF)
+
+    swap = remote(gathered, swapped, gt_sem.at[0], gt_sem.at[1], sec, partner)
+
+    def swap_parts(r, p):
+        id_swap.wait_recv()
+        back = way_back(targets(partner_ids[p // 2, p % 2, 0]))
+        span = half.at[r, pl.ds(0, 7)]
+        remote(span, span, pt_send.at[r, 0], pt_recv.at[r, 0], sec, partner).wait_recv()
+        for c in range(4):
+            gathered[:, pl.ds(c * CHUNK, CHUNK)] = rows_back(half.at[r], back, c).astype(BF)
+        swap.start()
+
+    def combine_swapped(r, p, read, index):
+        arrived(r)
+        swap.wait_recv()
+        for c in range(4):
+            cols = pl.ds(c * CHUNK, CHUNK)
+            both = rows_back(vals.at[r], pttab[p], c) + swapped[:, cols].astype(F32)
+            got = gtab[p][:, 0:1] * both.astype(BF).astype(F32)
             outs[index, :, cols] = (read(cols).astype(F32) + got).astype(BF)
 
     def from_tok(i):
@@ -324,6 +395,18 @@
     cot_two = choose(15, 4, 1)
     pass_left = remote(outs.at[0], passed.at[0], ps_sem.at[0, 0], ps_sem.at[1, 0], after, me)
     pass_right = remote(outs.at[1], passed.at[1], ps_sem.at[0, 1], ps_sem.at[1, 1], ahead, me)
+    def grads_of_inputs(i, carry):
+        cols = pl.ds(pl.multiple_of(i * 256, 256), 256)
+        total = dot_tn(xall[:, cols], dgu[...]).astype(BF)
+        gg_buf[cols, :] = total[:, :HALF]
+        gu_buf[cols, :] = total[:, HALF:]
+        return carry
+
+    def grads_of_down(i, carry):
+        cols = pl.ds(pl.multiple_of(i * 256, 256), 256)
+        gd_buf[:, cols] = dot_tn(hid[...], call[:, cols]).astype(BF)
+        return carry
+
     R_F0, R_B0, R_F1, R_B1, R_F2, R_B2 = range(6)
     loads[0].wait()
     gather(U_F0, F0, from_tok(0), False)
@@ -333,78 +416,68 @@
     gather(U_B1C, B1, from_tok(2), True)
 
     pl.semaphore_wait(barrier, 11)
-    for copy in mirrors:
-        copy.start()
-    ship(U_F0)
+    for i in (0, 1, 2, 3):
+        mirrors[i].start()
+    id_swap.start()
     ship(U_B1X)
     ship(U_B1C)
+    relay(U_B1X)
+    ship(U_F0)
     relay(U_F0)
-    relay(U_B1X)
     relay(U_B1C)
     for copy in loads[3:]:
         copy.wait()
-    expert_forward(U_F0, R_F0)
+    expert_forward(U_F0, R_F0, hand_over)
     mirrors[0].wait_recv()
     gather(U_B0C, B0, from_mir(0), True)
     ship(U_B0C)
     mirrors[1].wait_recv()
+    relay(U_B0C)
     gather(U_B0X, B0, from_mir(1), False)
     ship(U_B0X)
-    relay(U_B0C)
     relay(U_B0X)
+    add_halves(R_F0)
     expert_backward(U_B1X, U_B1C, 0, R_B1)
-    add_halves(R_F0)
     combine(R_F0, F0, from_tok(0), True, 0)
     pass_left.start()
     pass_left.wait_recv()
     gather(U_F2, F2, left_two, False)
     ship(U_F2)
     relay(U_F2)
-    expert_backward(U_B0X, U_B0C, 1, R_B0)
+    mirrors[2].wait_recv()
     add_halves(R_B1)
-    combine(R_B1, B1, from_tok(2), False, 3)
-    mirrors[2].wait_recv()
     gather(U_F1, F1, from_mir(2), False)
     ship(U_F1)
     mirrors[3].wait_recv()
+    expert_backward(U_B0X, U_B0C, 1, R_B0)
     gather(U_B2X, B2, from_mir(3), False)
     ship(U_B2X)
+    combine(R_B1, B1, from_tok(2), False, 3)
     relay(U_F1)
-    relay(U_B2X)
-    expert_forward(U_F2, R_F2)
+    expert_forward(U_F2, R_F2, hand_over)
     add_halves(R_B0)
     combine(R_B0, B0, from_mir(0), False, 1)
     pass_right.start()
     pass_right.wait_recv()
     gather(U_B2C, B2, cot_two, True)
     ship(U_B2C)
+    relay(U_B2X)
+    expert_forward(U_F1, R_F1, hand_out)
     relay(U_B2C)
-    expert_forward(U_F1, R_F1)
+    swap_parts(R_F1, F1)
     add_halves(R_F2)
     combine(R_F2, F2, left_two, True, 4)
     expert_backward(U_B2X, U_B2C, 2, R_B2)
-    add_halves(R_F1)
-    combine(R_F1, F1, from_mir(2), True, 2)
-
-    def grads_of_inputs(i, carry):
-        cols = pl.ds(pl.multiple_of(i * 256, 256), 256)
-        total = dot_tn(xall[:, cols], dgu[...]).astype(BF)
-        gg_buf[cols, :] = total[:, :HALF]
-        gu_buf[cols, :] = total[:, HALF:]
-        return carry
-
-    def grads_of_down(i, carry):
-        cols = pl.ds(pl.multiple_of(i * 256, 256), 256)
-        gd_buf[:, cols] = dot_tn(hid[...], call[:, cols]).astype(BF)
-        return carry
-
     lax.fori_loop(0, 8, grads_of_inputs, 0)
     add_halves(R_B2)
     lax.fori_loop(0, 8, grads_of_down, 0)
+    combine_swapped(R_F1, F1, from_mir(2), 2)
     combine(R_B2, B2, cot_two, False, 5)
 
     for copy in mirrors:
         copy.wait_send()
+    id_swap.wait_send()
+    swap.wait_send()
     pass_left.wait_send()
     pass_right.wait_send()
     for unit in range(9):
@@ -414,8 +487,9 @@
             span = recv.at[unit, pl.ds(4 * a, 4)]
             remote(span, span, rl_send.at[unit, a], rl_recv.at[unit, a], sec, partner).wait_send()
     for r in range(6):
-        span = part.at[r, pl.ds(8, 8)]
-        remote(span, span, pt_send.at[r], pt_recv.at[r], sec, partner).wait_send()
+        for a in range(1 if r == R_F1 else 2):
+            span = part.at[r, pl.ds(8, 7 if r == R_F1 else 4)]
+            remote(span, span, pt_send.at[r, a], pt_recv.at[r, a], sec, partner).wait_send()
         span = sums.at[r, pl.ds(0, 7)]
         remote(span, span, sm_send.at[r], sm_recv.at[r], sec, partner).wait_send()
 
@@ -487,6 +561,9 @@
         scratch_shapes=[
             pltpu.VMEM((3, 2, 1, 1, TOK), jnp.int32),
             pltpu.VMEM((3, 2, 1, 1, TOK), F32),
+            pltpu.VMEM((3, 2, 1, 1, TOK), jnp.int32),
+            pltpu.VMEM((TOK, D), BF),
+            pltpu.VMEM((TOK, D), BF),
             pltpu.VMEM((6, 128, TOK), BF),
             pltpu.VMEM((6, TOK, 128), BF),
             pltpu.VMEM((6, TOK, 128), F32),
@@ -512,11 +589,13 @@
             dma((9, 2)),
             dma((9, 2)),
             dma((9, 2)),
-            dma((6,)),
-            dma((6,)),
+            dma((6, 2)),
+            dma((6, 2)),
             dma((6,)),
             dma((6,)),
             dma((2, 2)),
+            dma((2,)),
+            dma((2,)),
         ],
         compiler_params=pltpu.CompilerParams(
             collective_id=0, has_side_effects=True, vmem_limit_bytes=60700000

time: 140 us -> 133 us (0.950)
  Pallas kernels: 139 us -> 132 us
    pallas_call x1, Pallas kernels: 136 us -> 129 us  [per_device(): pl.pallas_call(kernel, name='relay', out_shape=(pltpu.VMEM((6, TOK, D), B...]
where the time goes in v2:
time: 133 us
  Pallas kernels  132 us (99%)
    pallas_call x1, Pallas kernels, per_device(): pl.pallas_call(kernel, name='relay', out_shape=(pltpu.VMEM((6, TOK, D), B...  129 us
    pallas_call x1, Pallas kernels, per_device(): pl.pallas_call(write_out, name='write_out', out_shape=(sds((2, TOK, D), B...  2.73 us

profile of v2, /device:TPU:9, one launch (start us, length us, event | category | flops | bytes accessed | tf_op | source)
XLA Modules:
  0.0 132.9 jit_solution(18422645835506827515)
XLA Ops:
  0.6 129.3 %relay.1 = (bf16[6,64,2048]{2,1,0:T(8,128)(2,1)S(1)}, bf16[2048,384]{1,0:T(8,128)(2,1)S(1)}, bf16[2048,384]{1,0:T(8,128)(2,1)S(1)}, bf16[384,2048]{1,0:T(8,128)(2,1)S(1)}) custom-call(s32[3,2,1,1,64]{4,3,2,1,0:T(1,128)} %bitcast.13, f32[3,2,1,1,64]{4,3,2,1,0:T(1,128)} %bitcast.14, bf16[1,64,2048]{2,1,0:T(8,128)(2,1)} %left_in.1, bf16[64,2048]{1,0:T(8,128)(2,1)} %left_new.1, ...), custom_call_target="tpu_custom_call" | custom-call | tf_op jit(solution)/shard_map/relay/pallas_call | solution.py:550
  130.0 2.7 %write_out.1 = (bf16[2,64,2048]{2,1,0:T(8,128)(2,1)}, bf16[64,2048]{1,0:T(8,128)(2,1)}, bf16[64,2048]{1,0:T(8,128)(2,1)}, bf16[2,64,2048]{2,1,0:T(8,128)(2,1)}, ...) custom-call(bf16[6,64,2048]{2,1,0:T(8,128)(2,1)S(1)} %get-tuple-element.18.outs, ...), custom_call_target="tpu_custom_call" | custom-call | tf_op jit(solution)/shard_map/write_out/pallas_call | solution.py:618

commit v3 on v2

--- a/solution.py
+++ b/solution.py
@@ -303,7 +303,7 @@
         fold(r, lambda c: dot(hidden, wd[:, pl.ds(c * CHUNK, CHUNK)]))
         give(r)
 
-    def expert_backward(unit_x, unit_c, index, r):
+    def backward_inputs(unit_x, index):
         base = index * ROWS
         rows = pl.ds(base, ROWS)
         relayed(unit_x)
@@ -313,6 +313,12 @@
         logistic = jax.nn.sigmoid(gate)
         swish = gate * logistic
         hid[rows] = (swish * up).astype(BF)
+        return gate, up, logistic, swish
+
+    def backward_rest(unit_c, index, r, kept):
+        gate, up, logistic, swish = kept
+        base = index * ROWS
+        rows = pl.ds(base, ROWS)
         relayed(unit_c)
         unfold(unit_c, call, base)
         d_hidden = dot_nt(call[rows], wd[...])
@@ -322,6 +328,9 @@
         dgu[rows, pl.ds(HALF, HALF)] = d_up
         fold(r, lambda c: dot_nt(dgu[rows], wgu[pl.ds(c * CHUNK, CHUNK), :]))
         hand_over(r)
+
+    def expert_backward(unit_x, unit_c, index, r):
+        backward_rest(unit_c, index, r, backward_inputs(unit_x, index))
 
     def add_halves(r):
         for a in (1, 0):
@@ -416,7 +425,7 @@
     gather(U_B1C, B1, from_tok(2), True)
 
     pl.semaphore_wait(barrier, 11)
-    for i in (0, 1, 2, 3):
+    for i in (1, 0, 2, 3):
         mirrors[i].start()
     id_swap.start()
     ship(U_B1X)
@@ -428,14 +437,14 @@
     for copy in loads[3:]:
         copy.wait()
     expert_forward(U_F0, R_F0, hand_over)
+    mirrors[1].wait_recv()
+    gather(U_B0X, B0, from_mir(1), False)
+    ship(U_B0X)
+    relay(U_B0X)
     mirrors[0].wait_recv()
     gather(U_B0C, B0, from_mir(0), True)
     ship(U_B0C)
-    mirrors[1].wait_recv()
     relay(U_B0C)
-    gather(U_B0X, B0, from_mir(1), False)
-    ship(U_B0X)
-    relay(U_B0X)
     add_halves(R_F0)
     expert_backward(U_B1X, U_B1C, 0, R_B1)
     combine(R_F0, F0, from_tok(0), True, 0)
@@ -465,9 +474,10 @@
     expert_forward(U_F1, R_F1, hand_out)
     relay(U_B2C)
     swap_parts(R_F1, F1)
+    kept = backward_inputs(U_B2X, 2)
     add_halves(R_F2)
     combine(R_F2, F2, left_two, True, 4)
-    expert_backward(U_B2X, U_B2C, 2, R_B2)
+    backward_rest(U_B2C, 2, R_B2, kept)
     lax.fori_loop(0, 8, grads_of_inputs, 0)
     add_halves(R_B2)
     lax.fori_loop(0, 8, grads_of_down, 0)
@@ -508,10 +518,12 @@
     grad_down,
     sem,
 ):
-    pairs = [
-        (gg_buf, grad_gate),
-        (gu_buf, grad_up),
-        (gd_buf, grad_down),
+    pairs = []
+    for src, dst in ((gg_buf, grad_gate), (gu_buf, grad_up), (gd_buf, grad_down)):
+        count = src.shape[0] // 4
+        for i in range(4):
+            pairs.append((src.at[pl.ds(i * count, count)], dst.at[pl.ds(i * count, count)]))
+    pairs += [
         (outs.at[0], left_out.at[0]),
         (outs.at[1], right_back.at[0]),
         (outs.at[2], right_out),
@@ -629,7 +641,7 @@
         ),
         in_specs=[vmem] * 4,
         out_specs=(hbm,) * 7,
-        scratch_shapes=[dma((9,))],
+        scratch_shapes=[dma((18,))],
         compiler_params=pltpu.CompilerParams(vmem_limit_bytes=4 * 1024 * 1024),
     )(*results)
     return (

time: 133 us -> 133 us (level)
  no operation moved by 1% of the time
where the time goes in v3:
time: 133 us
  Pallas kernels  132 us (99%)
    pallas_call x1, Pallas kernels, per_device(): pl.pallas_call(kernel, name='relay', out_shape=(pltpu.VMEM((6, TOK, D), B...  129 us
    pallas_call x1, Pallas kernels, per_device(): pl.pallas_call(write_out, name='write_out', out_shape=(sds((2, TOK, D), B...  2.8 us

profile of v3, /device:TPU:9, one launch (start us, length us, event | category | flops | bytes accessed | tf_op | source)
XLA Modules:
  0.0 132.6 jit_solution(15205144367634322955)
XLA Ops:
  0.6 129.0 %relay.1 = (bf16[6,64,2048]{2,1,0:T(8,128)(2,1)S(1)}, bf16[2048,384]{1,0:T(8,128)(2,1)S(1)}, bf16[2048,384]{1,0:T(8,128)(2,1)S(1)}, bf16[384,2048]{1,0:T(8,128)(2,1)S(1)}) custom-call(s32[3,2,1,1,64]{4,3,2,1,0:T(1,128)} %bitcast.13, f32[3,2,1,1,64]{4,3,2,1,0:T(1,128)} %bitcast.14, bf16[1,64,2048]{2,1,0:T(8,128)(2,1)} %left_in.1, bf16[64,2048]{1,0:T(8,128)(2,1)} %left_new.1, ...), custom_call_target="tpu_custom_call" | custom-call | tf_op jit(solution)/shard_map/relay/pallas_call | solution.py:562
  129.7 2.8 %write_out.1 = (bf16[2,64,2048]{2,1,0:T(8,128)(2,1)}, bf16[64,2048]{1,0:T(8,128)(2,1)}, bf16[64,2048]{1,0:T(8,128)(2,1)}, bf16[2,64,2048]{2,1,0:T(8,128)(2,1)}, ...) custom-call(bf16[6,64,2048]{2,1,0:T(8,128)(2,1)S(1)} %get-tuple-element.18.outs, ...), custom_call_target="tpu_custom_call" | custom-call | tf_op jit(solution)/shard_map/write_out/pallas_call | solution.py:630
